TPU v7x, 32 devices: a whole 2x2x4 slice. The times are simulated.
32 devices in a mesh: strip: 4 (over z), date: 8 (over y, x, core).
Axes of the slice: x: 2, y: 2, z: 4, core: 2. Of those that a mesh axis runs over, the one named last changes fastest.
Arguments:
- images: bfloat16 [128, 256, 128], P('date', 'strip'), may hold values from 0.19921875 to 5
- inverse_blocks: float32 [2, 8, 128, 128], P(None, 'strip', 'date'), as said below
- pair_first: int32 [256], P('date'), may hold values from 0 to 15
- pair_block: int32 [256, 1], P('date'), may hold values from 0 to 7; in each aligned block of 32 rows (0 to 31, 32 to 63, ...) at most 8 rows name the same one
- pair_second: int32 [256], P('date'), may hold values from 0 to 15
- pair_count: int32 [8], P('date'), may hold values from 8 to 32, as said below
- shifts: int32 [256, 2, 8], P('date', None, 'strip'), may hold values from -8 to 8
- anchors: int32 [8], P('strip'), may hold values from 0 to 96, as said below
Outputs:
- pair_offsets: float32 [256, 2, 8], P('date', None, 'strip')
- series: float32 [2, 8, 128], P(None, 'strip', 'date')
Inputs may be any that keep to these rules, and one draw needn't show every extreme that they name: `pair_block`: among the 32 slots of one date block at most 8 name one partner block, and some block is named that often. `pair_count`: slots 0 to count - 1 of a date block are live; slots at or past the count carry no pair, and their partner windows need not be sent. One block has all 32 live, one has 8, every other block 24 or more. `anchors`: chip q starts at column (q % 2) * 64 plus 0 to 32. `inverse_blocks`: symmetric in its last two dimensions.
All inputs are finite; a program needn't handle non-finite values.
Results may differ from a plain program's by a relative error of at most 0.008.
Values may be sent and summed in bfloat16 or wider, within the bound.
A program may use at most 64 MiB of HBM per device.

v0:
```python
import math
import jax
import jax.numpy as jnp
from jax import lax
from jax.sharding import PartitionSpec as P

SMAX = 8


def padded(cells, sides, width):
    for axis, dim in sides:
        count = lax.axis_size(axis)
        ends = count - 1
        head = lax.slice_in_dim(cells, 0, width, axis=dim)
        tail = lax.slice_in_dim(cells, cells.shape[dim] - width, cells.shape[dim], axis=dim)
        cells = jnp.concatenate(
            [
                lax.ppermute(tail, axis, [(i, (i + 1) % count) for i in range(ends)]),
                cells,
                lax.ppermute(head, axis, [((i + 1) % count, i) for i in range(ends)]),
            ],
            axis=dim,
        )
    return cells


def make_tables(length):
    counter = jnp.arange(length, dtype=jnp.int32)
    products = counter[:, None] * counter[None, :] % length
    radians = products.astype(jnp.float32) * (2.0 * math.pi / length)
    cosine = jnp.cos(radians)
    sine_part = -jnp.sin(radians)
    forward = jnp.concatenate([cosine, sine_part], axis=1).astype(jnp.bfloat16)
    over_len = 2 * length
    signed = jnp.where(counter < length // 2, counter, counter - length)
    places = jnp.arange(over_len, dtype=jnp.int32)
    turned = signed[:, None] * places[None, :] % over_len
    angles = turned.astype(jnp.float32) * (2.0 * math.pi / over_len)
    vcosine = jnp.cos(angles)
    vsine = jnp.sin(angles)
    top_rows = jnp.concatenate([vcosine, vsine], axis=1)
    low_rows = jnp.concatenate([-vsine, vcosine], axis=1)
    inverse_rows = jnp.concatenate([top_rows, low_rows], axis=0).astype(jnp.bfloat16)
    displace = ((places + length) % over_len - length).astype(jnp.float32) * 0.5
    return (
        forward,
        cosine.astype(jnp.bfloat16),
        sine_part.astype(jnp.bfloat16),
        inverse_rows,
        vcosine.T.astype(jnp.bfloat16),
        vsine.T.astype(jnp.bfloat16),
        displace,
    )


def spectra(windows, tables):
    forward, cosine_b, sine_b = (tables[0], tables[1], tables[2])
    length = windows.shape[-1]
    values = windows.astype(jnp.float32)
    centred = (values - jnp.mean(values, axis=(1, 2), keepdims=True)).astype(jnp.bfloat16)
    section_one = jnp.einsum(
        "bmn,nk->bmk", centred, forward, preferred_element_type=jnp.float32
    ).astype(jnp.bfloat16)
    with_cos = jnp.einsum("km,bmj->bkj", cosine_b, section_one, preferred_element_type=jnp.float32)
    with_sin = jnp.einsum("km,bmj->bkj", sine_b, section_one, preferred_element_type=jnp.float32)
    real_part = with_cos[:, :, :length] - with_sin[:, :, length:]
    imag_part = with_sin[:, :, :length] + with_cos[:, :, length:]
    return jnp.concatenate([real_part, imag_part], axis=2).astype(jnp.bfloat16)


def centroid(near_spec, far_spec, tables):
    inverse_rows, back_cos, back_sin, displace = (tables[3], tables[4], tables[5], tables[6])
    length = near_spec.shape[-1] // 2
    near_re = near_spec[:, :, :length].astype(jnp.float32)
    near_im = near_spec[:, :, length:].astype(jnp.float32)
    far_re = far_spec[:, :, :length].astype(jnp.float32)
    far_im = far_spec[:, :, length:].astype(jnp.float32)
    cross_re = near_re * far_re + near_im * far_im
    cross_im = near_im * far_re - near_re * far_im
    cross_spec = jnp.concatenate([cross_re, cross_im], axis=2).astype(jnp.bfloat16)
    along = jnp.einsum(
        "bun,nl->bul", cross_spec, inverse_rows, preferred_element_type=jnp.float32
    ).astype(jnp.bfloat16)
    half_width = along.shape[-1] // 2
    surface = jnp.einsum(
        "ku,bul->bkl", back_cos, along[:, :, :half_width], preferred_element_type=jnp.float32
    )
    surface = surface - jnp.einsum(
        "ku,bul->bkl", back_sin, along[:, :, half_width:], preferred_element_type=jnp.float32
    )
    energy = surface * surface
    norm_val = jnp.mean(energy, axis=(1, 2)) + 1e-06
    row_shift = jnp.mean(energy * displace[None, :, None], axis=(1, 2)) / norm_val
    col_shift = jnp.mean(energy * displace[None, None, :], axis=(1, 2)) / norm_val
    return jnp.stack([row_shift, col_shift], axis=1)


def body(images, inverse_blocks, pair_first, pair_block, pair_second, pair_count, shifts, anchors):
    devices = lax.axis_size("date")
    block_id = lax.axis_index("date")
    dates_dev, length, columns = images.shape
    pair_dev = pair_first.shape[0]
    chip_count = anchors.shape[0]
    capacity = max(2, 2 * pair_dev // devices)
    margin = SMAX
    extent = length + 2 * margin
    tables = make_tables(length)
    target = pair_block[:, 0]
    hit_table = (target[:, None] == jnp.arange(devices, dtype=jnp.int32)[None, :]).astype(jnp.int32)
    earlier = jnp.cumsum(hit_table, axis=0) - hit_table
    rank_in = jnp.sum(earlier * hit_table, axis=1)
    slot_of = target * capacity + rank_in
    requests = (
        jnp.zeros((devices * capacity,), jnp.int32)
        .at[slot_of]
        .set(pair_second)
        .reshape(devices, capacity)
    )
    asked_for = lax.all_to_all(requests, "date", split_axis=0, concat_axis=0, tiled=True)
    wanted = asked_for.reshape(-1)
    picked = jnp.take(images, wanted, axis=0).reshape(devices, capacity, length, columns)
    arrived = lax.all_to_all(picked, "date", split_axis=0, concat_axis=0, tiled=True)
    framed = padded(arrived, (("strip", 2),), margin)
    framed = framed.reshape(devices * capacity, extent, columns)
    framed = jnp.pad(framed, ((0, 0), (0, 0), (margin, margin + length // 2)))
    own_pad = jnp.pad(images, ((0, 0), (0, 0), (0, length // 2)))
    own_list = []
    region_list = []
    for chip_one in range(chip_count):
        own_list.append(lax.dynamic_slice_in_dim(own_pad, anchors[chip_one], length, 2))
        region_list.append(lax.dynamic_slice_in_dim(framed, anchors[chip_one], extent, 2))
    own_windows = jnp.stack(own_list, axis=1)
    regions = jnp.stack(region_list, axis=1)
    own_spec = spectra(own_windows.reshape(-1, length, length), tables).reshape(
        dates_dev, chip_count, length, 2 * length
    )
    step_pairs = math.gcd(pair_dev, max(1, 512 // chip_count))
    turn_count = pair_dev // step_pairs
    inside = jnp.arange(length, dtype=jnp.int32)
    across = jnp.arange(extent, dtype=jnp.int32)

    def one_turn(packed):
        slots_turn, firsts_turn, shifts_turn = packed
        regions_turn = jnp.take(regions, slots_turn, axis=0)
        row_start = margin + shifts_turn[:, 0, :]
        col_start = margin + shifts_turn[:, 1, :]
        row_pick = (
            across[None, None, None, :] == row_start[:, :, None, None] + inside[None, None, :, None]
        ).astype(jnp.bfloat16)
        col_pick = (
            across[None, None, :, None] == col_start[:, :, None, None] + inside[None, None, None, :]
        ).astype(jnp.bfloat16)
        row_cut = jnp.einsum(
            "pcie,pcef->pcif", row_pick, regions_turn, preferred_element_type=jnp.float32
        ).astype(jnp.bfloat16)
        far_windows = jnp.einsum(
            "pcif,pcfj->pcij", row_cut, col_pick, preferred_element_type=jnp.float32
        ).astype(jnp.bfloat16)
        far_spec = spectra(far_windows.reshape(-1, length, length), tables)
        near_spec = jnp.take(own_spec, firsts_turn, axis=0).reshape(-1, length, 2 * length)
        return centroid(near_spec, far_spec, tables).reshape(step_pairs, chip_count, 2)

    packed = (
        slot_of.reshape(turn_count, step_pairs),
        pair_first.reshape(turn_count, step_pairs),
        shifts.reshape(turn_count, step_pairs, 2, chip_count),
    )
    centroids = lax.map(one_turn, packed).reshape(pair_dev, chip_count, 2)
    live_mask = (jnp.arange(pair_dev, dtype=jnp.int32) < pair_count[0]).astype(jnp.float32)
    pair_offsets = (shifts.astype(jnp.float32) + jnp.swapaxes(centroids, 1, 2)) * live_mask[
        :, None, None
    ]
    dates_all = dates_dev * devices
    date_ids = jnp.arange(dates_all, dtype=jnp.int32)
    second_id = target * dates_dev + pair_second
    first_id = block_id * dates_dev + pair_first
    incidence = (second_id[:, None] == date_ids[None, :]).astype(jnp.float32) - (
        first_id[:, None] == date_ids[None, :]
    ).astype(jnp.float32)
    partial_value = jnp.einsum(
        "pxc,pd->xcd", pair_offsets, incidence, precision=lax.Precision.HIGHEST
    )
    rhs_whole = lax.psum(partial_value, "date")
    series = jnp.einsum("xcde,xce->xcd", inverse_blocks, rhs_whole, precision=lax.Precision.HIGHEST)
    return (pair_offsets, series)


def solution(mesh):
    return jax.shard_map(
        body,
        mesh=mesh,
        in_specs=(
            P("date", "strip", None),
            P(None, "strip", "date", None),
            P("date"),
            P("date", None),
            P("date"),
            P("date"),
            P("date", None, "strip"),
            P("strip"),
        ),
        out_specs=(P("date", None, "strip"), P(None, "strip", "date")),
        check_vma=False,
    )
```

profile of v0, /device:TPU:0, one launch (start us, length us, event | category | flops | bytes accessed | tf_op | source)
XLA Modules:
  0.0 84.8 jit_solution(15809964024096351249)
XLA Ops:
  1.4 0.8 select_reduce_fusion
  2.9 0.8 scatter_custom_fusion
  4.4 5.2 %all-to-all-start = ((s32[8,1,8]{2,1,0:T(1,128)}), s32[8,1,8]{2,1,0:T(1,128)S(1)}, u32[]{:S(2)}, u32[]{:S(2)}) async-start(s32[8,1,8]{2,1,0:T(1,128)} %bitcast.18), calls=%async_computation | async-start | bytes 8192 | tf_op jit(solution)/shard_map/all_to_all | solution.py:119
  9.8 1.3 %fusion.120 = (s32[1]{0:T(128)}, s32[1]{0:T(128)}) fusion(s32[2]{0:T(128)} %param.15), kind=kLoop, calls=%fused_computation.195 | loop fusion | bytes 16 | tf_op jit(solution)/shard_map/slice | solution.py:131
  15.0 1.3 %fusion.32 = (bf16[16,1,64,64]{3,2,1,0:T(8,128)(2,1)S(1)}, bf16[16,1,64,64]{3,2,1,0:T(8,128)(2,1)S(1)}) fusion(s32[]{:T(128)S(6)} %select_n.129, bf16[16,64,128]{2,1,0:T(8,128)(2,1)} %param.8, s32[]{:T(128)S(6)} %select_n.130), kind=kLoop, calls=%fused_computation.64 | loop fusion | bytes 524296 | tf_op jit(solution)/shard_map/stack | solution.py:132
  20.1 0.7 gather_fusion
  22.3 0.7 gather_fusion.1
  23.1 1.2 %broadcast_select_fusion = bf16[8,8,64,128]{3,2,1,0:T(8,128)(2,1)} fusion(bf16[8,8,64,128]{3,2,1,0:T(8,128)(2,1)S(1)} %bitcast.101, pred[8,8]{1,0:T(8,128)(4,1)S(1)} %compare_and_fusion), kind=kLoop, calls=%fused_computation.58 | loop fusion | flops 524288 | bytes 2097216 | tf_op jit(solution)/shard_map/jit(_take)/select_n | solution.py:121
  24.2 4.2 %all-to-all-start.1 = ((bf16[8,8,64,128]{3,2,1,0:T(8,128)(2,1)}), bf16[8,8,64,128]{3,2,1,0:T(8,128)(2,1)S(1)}, u32[]{:S(2)}, u32[]{:S(2)}) async-start(bf16[8,8,64,128]{3,2,1,0:T(8,128)(2,1)} %broadcast_select_fusion), calls=%async_computation.1 | async-start | bytes 2097152 | tf_op jit(solution)/shard_map/all_to_all | solution.py:122
  29.1 14.8 %all-to-all-done.1 = bf16[8,8,64,128]{3,2,1,0:T(8,128)(2,1)S(1)} async-done(((bf16[8,8,64,128]{3,2,1,0:T(8,128)(2,1)}), bf16[8,8,64,128]{3,2,1,0:T(8,128)(2,1)S(1)}, u32[]{:S(2)}, u32[]{:S(2)}) %all-to-all-start.1) | async-done | bytes 1048608 | tf_op jit(solution)/shard_map/all_to_all | solution.py:122
  43.9 3.5 %collective-permute-start = (bf16[8,8,8,128]{3,2,1,0:T(8,128)(2,1)S(1)}, bf16[8,8,8,128]{3,2,1,0:T(8,128)(2,1)S(1)}, u32[]{:S(2)}, u32[]{:S(2)}) collective-permute-start(bf16[8,8,8,128]{3,2,1,0:T(8,128)(2,1)S(1)} %get-tuple-element.68), channel_id=1, source_target_pairs={{0,8},{8,16},{16,24},{1,9},{9,17},{17,25},{2,10},{10,18},{18,26},{... | collective-permute-start | bytes 393224 | tf_op jit(solution)/shard_map/ppermute | solution.py:18
  47.4 1.5 %collective-permute-start.1 = (bf16[8,8,8,128]{3,2,1,0:T(8,128)(2,1)S(1)}, bf16[8,8,8,128]{3,2,1,0:T(8,128)(2,1)S(1)}, u32[]{:S(2)}, u32[]{:S(2)}) collective-permute-start(bf16[8,8,8,128]{3,2,1,0:T(8,128)(2,1)S(1)} %get-tuple-element.69), channel_id=1, source_target_pairs={{8,0},{16,8},{24,16},{9,1},{17,9},{25,17},{10,2},{18,10},{26,18},{... | collective-permute-start | bytes 393224 | tf_op jit(solution)/shard_map/ppermute | solution.py:20
  51.5 2.8 %collective-permute-done.1 = bf16[8,8,8,128]{3,2,1,0:T(8,128)(2,1)S(1)} collective-permute-done((bf16[8,8,8,128]{3,2,1,0:T(8,128)(2,1)S(1)}, bf16[8,8,8,128]{3,2,1,0:T(8,128)(2,1)S(1)}, u32[]{:S(2)}, u32[]{:S(2)}) %collective-permute-start.1) | collective-permute-done | bytes 131104 | tf_op jit(solution)/shard_map/ppermute | solution.py:20
  54.4 1.1 %fusion.12 = (bf16[64,1,80,80]{3,2,0,1:T(8,128)(2,1)S(1)}, bf16[64,1,80,80]{3,2,0,1:T(8,128)(2,1)S(1)}) fusion(s32[]{:T(128)S(6)} %select_n.137, bf16[64,80,128]{2,1,0:T(8,128)(2,1)S(1)} %bitcast.100, s32[]{:T(128)S(6)} %select_n.138), kind=kLoop, calls=%fused_computation.37 | loop fusion | bytes 2949128 | tf_op jit(solution)/shard_map/stack | solution.py:133
  55.5 2.1 %pad_maximum_fusion = bf16[64,2,80,80]{3,2,0,1:T(8,128)(2,1)} fusion(bf16[64,1,80,80]{3,2,0,1:T(8,128)(2,1)S(1)} %get-tuple-element.67, bf16[64,1,80,80]{3,2,0,1:T(8,128)(2,1)S(1)} %get-tuple-element.66), kind=kLoop, calls=%fused_computation.13 | loop fusion | flops 819200 | bytes 3276800 | tf_op jit(solution)/shard_map/stack | solution.py:133
  57.6 3.5 %gather_fusion.2 = bf16[32,2,80,80]{3,2,1,0:T(8,128)(2,1)} fusion(bf16[64,2,80,80]{3,2,0,1:T(8,128)(2,1)} %pad_maximum_fusion, s32[1024]{0:T(1024)S(1)} %pad_clamp_fusion), kind=kCustom, calls=%fused_computation.2 | custom fusion | bytes 1638528 | tf_op jit(solution)/shard_map/while/body/eval_jaxpr/jit(_take)/gather | solution.py:144
  61.1 2.8 %fusion.121 = (f32[32,2]{1,0:T(8,128)S(1)}, f32[32,2,64,64]{3,2,1,0:T(8,128)S(1)}) fusion(s32[32,2,64]{2,1,0:T(2,128)S(1)} %get-tuple-element.87, bf16[32,2,80,80]{3,2,1,0:T(8,128)(2,1)} %gather_fusion.2, pred[32]{0:T(512)(128)(4,1)S(1)} %get-tuple-element.46, s32[32,2,64]{2,1,0:T(2,128)S(1)} %get-tuple-element.88), kind=kOutput, calls=%fused_computation.196 | convolution fusion | flops 96550848 | bytes 1900832 | tf_op jit(solution)/shard_map/while/body/eval_jaxpr/pcif,pcfj->pcij/dot_general | solution.py:156
  65.8 1.5 %fusion.1 = (bf16[64,64,64]{2,1,0:T(8,128)(2,1)S(1)}, bf16[64,64,64]{2,1,0:T(8,128)(2,1)S(1)}, bf16[64,64,64]{2,1,0:T(8,128)(2,1)S(1)}) fusion(bf16[64,64,128]{2,1,0:T(8,128)(2,1)S(1)} %bitcast_select_fusion, f32[64,64,128]{2,1,0:T(8,128)S(1)} %convolution_bitcast_fusion.1, f32[64,64,128]{2,1,0:T(8,128)S(1)} %convolution_bitcast_fusion), kind=kLoop, calls=%fused_computation.15 | loop fusion | flops 3145728 | bytes 6815744 | tf_op jit(solution)/shard_map/convert.8
  67.3 0.8 fusion.3
  68.1 0.8 convolution_convert_fusion
  68.9 0.9 %fusion.19 = f32[64,128,128]{2,1,0:T(8,128)S(1)} fusion(bf16[64,64,256]{2,1,0:T(8,128)(2,1)S(1)} %convolution_convert_fusion, s32[64]{0:T(128)S(1)} %compare_select_fusion.1), kind=kOutput, calls=%fused_computation.44 | convolution fusion | flops 134340608 | bytes 5243392 | tf_op jit(solution)/shard_map/while/body/eval_jaxpr/ku,bul->bkl/dot_general | solution.py:85
  69.8 1.9 %multiply_reduce_fusion.1 = (f32[64]{0:T(128)S(1)}, f32[64]{0:T(128)S(1)}, f32[64]{0:T(128)S(1)}) fusion(f32[128]{0:T(128)S(1)} %fusion.89, f32[64,128,128]{2,1,0:T(8,128)S(1)} %fusion.19, s32[64]{0:T(128)S(1)} %compare_select_fusion.1, bf16[64,64,256]{2,1,0:T(8,128)(2,1)S(1)} %convolution_convert_fusion), kind=kOutput, calls=%fused_computation.5 | convolution fusion | flops 141680448 | bytes 5245184 | tf_op jit(solution)/shard_map/while/body/eval_jaxpr/ku,bul->bkl/dot_general | solution.py:88
  72.3 11.8 %psum.7 = f32[2,2,128]{2,1,0:T(2,128)S(1)} all-reduce(f32[2,2,128]{2,1,0:T(2,128)S(1)} %fusion.63), channel_id=1, replica_groups=mesh['strip'=4,'date'=8] {'date'}, use_global_device_ids=true, to_apply=%region_8.9 | all-reduce | flops 512 | bytes 4096 | tf_op jit(solution)/shard_map/psum | solution.py:183
  84.1 0.7 fusion.124
  (69 shorter events, 10.1 us)
Async XLA Ops:
  0.6 83.5 %copy-start = (f32[2,2,16,128]{3,2,1,0:T(8,128)S(1)}, f32[2,2,16,128]{3,2,1,0:T(8,128)}, u32[]{:S(2)}) copy-start(f32[2,2,16,128]{3,2,1,0:T(8,128)} %param.9) | copy-start | bytes 98308
  4.4 16.4 %all-to-all-start = ((s32[8,1,8]{2,1,0:T(1,128)}), s32[8,1,8]{2,1,0:T(1,128)S(1)}, u32[]{:S(2)}, u32[]{:S(2)}) async-start(s32[8,1,8]{2,1,0:T(1,128)} %bitcast.18), calls=%async_computation | async-start | bytes 8192 | tf_op jit(solution)/shard_map/all_to_all | solution.py:119
  16.9 1.2 %copy-start.2 = (s32[32,2,2]{0,2,1:T(2,128)S(1)}, s32[32,2,2]{0,2,1:T(2,128)}, u32[]{:S(2)}) copy-start(s32[32,2,2]{0,2,1:T(2,128)} %param.14) | copy-start | bytes 1540
  16.9 1.4 %copy-start.5 = (s32[32]{0:T(128)S(1)}, s32[32]{0:T(128)}, u32[]{:S(2)}) copy-start(s32[32]{0:T(128)} %param.10) | copy-start | bytes 388
  19.0 3.3 %copy-start.1 = (bf16[16,64,128]{2,1,0:T(8,128)(2,1)S(1)}, bf16[16,64,128]{2,1,0:T(8,128)(2,1)}, u32[]{:S(2)}) copy-start(bf16[16,64,128]{2,1,0:T(8,128)(2,1)} %param.8) | copy-start | bytes 786436
  23.1 5.4 %copy-start.3 = (s32[32,1]{0,1:T(1,128)S(1)}, s32[32,1]{0,1:T(1,128)}, u32[]{:S(2)}) copy-start(s32[32,1]{0,1:T(1,128)} %param.11) | copy-start | bytes 388
  23.1 5.4 %copy-start.6 = (s32[32]{0:T(128)S(1)}, s32[32]{0:T(128)}, u32[]{:S(2)}) copy-start(s32[32]{0:T(128)} %param.12) | copy-start | bytes 388
  24.2 19.6 %all-to-all-start.1 = ((bf16[8,8,64,128]{3,2,1,0:T(8,128)(2,1)}), bf16[8,8,64,128]{3,2,1,0:T(8,128)(2,1)S(1)}, u32[]{:S(2)}, u32[]{:S(2)}) async-start(bf16[8,8,64,128]{3,2,1,0:T(8,128)(2,1)} %broadcast_select_fusion), calls=%async_computation.1 | async-start | bytes 2097152 | tf_op jit(solution)/shard_map/all_to_all | solution.py:122
  43.9 7.6 %collective-permute-start = (bf16[8,8,8,128]{3,2,1,0:T(8,128)(2,1)S(1)}, bf16[8,8,8,128]{3,2,1,0:T(8,128)(2,1)S(1)}, u32[]{:S(2)}, u32[]{:S(2)}) collective-permute-start(bf16[8,8,8,128]{3,2,1,0:T(8,128)(2,1)S(1)} %get-tuple-element.68), channel_id=1, source_target_pairs={{0,8},{8,16},{16,24},{1,9},{9,17},{17,25},{2,10},{10,18},{18,26},{... | collective-permute-start | bytes 393224 | tf_op jit(solution)/shard_map/ppermute | solution.py:18
  47.4 6.9 %collective-permute-start.1 = (bf16[8,8,8,128]{3,2,1,0:T(8,128)(2,1)S(1)}, bf16[8,8,8,128]{3,2,1,0:T(8,128)(2,1)S(1)}, u32[]{:S(2)}, u32[]{:S(2)}) collective-permute-start(bf16[8,8,8,128]{3,2,1,0:T(8,128)(2,1)S(1)} %get-tuple-element.69), channel_id=1, source_target_pairs={{8,0},{16,8},{24,16},{9,1},{17,9},{25,17},{10,2},{18,10},{26,18},{... | collective-permute-start | bytes 393224 | tf_op jit(solution)/shard_map/ppermute | solution.py:20
  72.1 12.8 %copy-start.4 = (f32[32,2,2]{0,2,1:T(2,128)}, f32[32,2,2]{0,2,1:T(2,128)S(1)}, u32[]{:S(2)}) copy-start(f32[32,2,2]{0,2,1:T(2,128)S(1)} %copy.25) | copy-start | bytes 1540
where the time goes:
time: 85.4 us; the launch traced here: 84.8 us
  waiting for transfers between devices  17.5 us (20%)
  starting transfers between devices  14.4 us (17%)
  local copies, waits for them, and re-layouts  11.9 us (14%)
  blocking collectives  11.8 us (14%)
  other arithmetic  11.2 us (13%)
  matrix products  9.92 us (12%)
  between operations  8.17 us (10%)
    all_to_all x1, waiting for transfers between devices, body(): lax.all_to_all(picked, 'date', split_axis=0, concat_axis=0, tiled=True)  14.8 us
    psum x1, blocking collectives, body(): rhs_whole = lax.psum(partial_value, 'date')  11.8 us
    all_to_all x1, starting transfers between devices, body(): lax.all_to_all(requests, 'date', split_axis=0, concat_axis=0, tiled=True)  5.2 us
    all_to_all x1, starting transfers between devices, body(): lax.all_to_all(picked, 'date', split_axis=0, concat_axis=0, tiled=True)  4.2 us
    gather x1, local copies, waits for them, and re-layouts, one_turn(): regions_turn = jnp.take(regions, slots_turn, axis=0)  3.54 us
    ppermute x1, starting transfers between devices, padded(): lax.ppermute(tail, axis, [(i, (i + 1) % count) for i in range(ends)])  3.49 us
    another operation x5, other arithmetic  3.26 us
    ppermute x1, waiting for transfers between devices, padded(): lax.ppermute(head, axis, [((i + 1) % count, i) for i in range(ends)])  2.76 us
  transfers between devices with their start and end apart: 4, of which 2 were waited for; matrix products, arithmetic and copies ran while one was open for 8% of the time, Pallas kernels for 0%

commit v1 on v0

--- a/solution.py
+++ b/solution.py
@@ -180,7 +180,11 @@
     partial_value = jnp.einsum(
         "pxc,pd->xcd", pair_offsets, incidence, precision=lax.Precision.HIGHEST
     )
-    rhs_whole = lax.psum(partial_value, "date")
+
+    def list_shelves(q_in):
+        return lax.all_gather(q_in, "date").sum(axis=0)
+
+    rhs_whole = list_shelves(partial_value)
     series = jnp.einsum("xcde,xce->xcd", inverse_blocks, rhs_whole, precision=lax.Precision.HIGHEST)
     return (pair_offsets, series)
 

time: 85.4 us -> 81.8 us (0.958)
  blocking collectives: 11.8 us -> 8.14 us
    psum x1 -> x0, blocking collectives: 11.8 us -> none  [body(): rhs_whole = lax.psum(partial_value, 'date')]
    all_gather x0 -> x1, blocking collectives: none -> 8.14 us  [list_shelves(): return lax.all_gather(q_in, 'date').sum(axis=0)]
  transfers between devices with their start and end apart: 4 -> 4, of which waited for: 2 -> 2; matrix products, arithmetic and copies ran while one was open for 8% -> 9% of each run, Pallas kernels for 0% -> 0%
where the time goes in v1:
time: 81.8 us; the launch traced here: 81.2 us
  waiting for transfers between devices  17.5 us (21%)
  starting transfers between devices  14.4 us (18%)
  local copies, waits for them, and re-layouts  11.9 us (15%)
  other arithmetic  11.2 us (14%)
  matrix products  9.92 us (12%)
  between operations  8.18 us (10%)
  blocking collectives  8.14 us (10%)
    all_to_all x1, waiting for transfers between devices, body(): lax.all_to_all(picked, 'date', split_axis=0, concat_axis=0, tiled=True)  14.8 us
    all_gather x1, blocking collectives, list_shelves(): return lax.all_gather(q_in, 'date').sum(axis=0)  8.14 us
    all_to_all x1, starting transfers between devices, body(): lax.all_to_all(requests, 'date', split_axis=0, concat_axis=0, tiled=True)  5.2 us
    all_to_all x1, starting transfers between devices, body(): lax.all_to_all(picked, 'date', split_axis=0, concat_axis=0, tiled=True)  4.2 us
    gather x1, local copies, waits for them, and re-layouts, one_turn(): regions_turn = jnp.take(regions, slots_turn, axis=0)  3.54 us
    ppermute x1, starting transfers between devices, padded(): lax.ppermute(tail, axis, [(i, (i + 1) % count) for i in range(ends)])  3.49 us
    another operation x5, other arithmetic  3.26 us
    ppermute x1, waiting for transfers between devices, padded(): lax.ppermute(head, axis, [((i + 1) % count, i) for i in range(ends)])  2.76 us
  transfers between devices with their start and end apart: 4, of which 2 were waited for; matrix products, arithmetic and copies ran while one was open for 9% of the time, Pallas kernels for 0%

profile of v1, /device:TPU:0, one launch (start us, length us, event | category | flops | bytes accessed | tf_op | source)
XLA Modules:
  0.0 81.2 jit_solution(1901929643984415560)
XLA Ops:
  1.4 0.8 %select_reduce_fusion = s32[32]{0:T(128)S(1)} fusion(s32[32,8]{1,0:T(8,128)S(1)} %reduce_window_sum.11, s32[32]{0:T(128)} %bitcast.109), kind=kLoop, calls=%fused_computation.125 | loop fusion | flops 1248 | bytes 1280 | tf_op jit(solution)/shard_map/reduce_sum | solution.py:111
  2.9 0.8 scatter_custom_fusion
  4.4 5.2 %all-to-all-start = ((s32[8,1,8]{2,1,0:T(1,128)}), s32[8,1,8]{2,1,0:T(1,128)S(1)}, u32[]{:S(2)}, u32[]{:S(2)}) async-start(s32[8,1,8]{2,1,0:T(1,128)} %bitcast.18), calls=%async_computation | async-start | bytes 8192 | tf_op jit(solution)/shard_map/all_to_all | solution.py:119
  9.8 1.3 %fusion.120 = (s32[1]{0:T(128)}, s32[1]{0:T(128)}) fusion(s32[2]{0:T(128)} %param.15), kind=kLoop, calls=%fused_computation.195 | loop fusion | bytes 16 | tf_op jit(solution)/shard_map/slice | solution.py:131
  15.0 1.3 %fusion.32 = (bf16[16,1,64,64]{3,2,1,0:T(8,128)(2,1)S(1)}, bf16[16,1,64,64]{3,2,1,0:T(8,128)(2,1)S(1)}) fusion(s32[]{:T(128)S(6)} %select_n.129, bf16[16,64,128]{2,1,0:T(8,128)(2,1)} %param.8, s32[]{:T(128)S(6)} %select_n.130), kind=kLoop, calls=%fused_computation.64 | loop fusion | bytes 524296 | tf_op jit(solution)/shard_map/stack | solution.py:132
  20.1 0.7 gather_fusion
  22.3 0.7 gather_fusion.1
  23.1 1.2 %broadcast_select_fusion = bf16[8,8,64,128]{3,2,1,0:T(8,128)(2,1)} fusion(bf16[8,8,64,128]{3,2,1,0:T(8,128)(2,1)S(1)} %bitcast.102, pred[8,8]{1,0:T(8,128)(4,1)S(1)} %compare_and_fusion), kind=kLoop, calls=%fused_computation.58 | loop fusion | flops 524288 | bytes 2097216 | tf_op jit(solution)/shard_map/jit(_take)/select_n | solution.py:121
  24.2 4.2 %all-to-all-start.1 = ((bf16[8,8,64,128]{3,2,1,0:T(8,128)(2,1)}), bf16[8,8,64,128]{3,2,1,0:T(8,128)(2,1)S(1)}, u32[]{:S(2)}, u32[]{:S(2)}) async-start(bf16[8,8,64,128]{3,2,1,0:T(8,128)(2,1)} %broadcast_select_fusion), calls=%async_computation.1 | async-start | bytes 2097152 | tf_op jit(solution)/shard_map/all_to_all | solution.py:122
  29.1 14.8 %all-to-all-done.1 = bf16[8,8,64,128]{3,2,1,0:T(8,128)(2,1)S(1)} async-done(((bf16[8,8,64,128]{3,2,1,0:T(8,128)(2,1)}), bf16[8,8,64,128]{3,2,1,0:T(8,128)(2,1)S(1)}, u32[]{:S(2)}, u32[]{:S(2)}) %all-to-all-start.1) | async-done | bytes 1048608 | tf_op jit(solution)/shard_map/all_to_all | solution.py:122
  43.9 3.5 %collective-permute-start = (bf16[8,8,8,128]{3,2,1,0:T(8,128)(2,1)S(1)}, bf16[8,8,8,128]{3,2,1,0:T(8,128)(2,1)S(1)}, u32[]{:S(2)}, u32[]{:S(2)}) collective-permute-start(bf16[8,8,8,128]{3,2,1,0:T(8,128)(2,1)S(1)} %get-tuple-element.68), channel_id=1, source_target_pairs={{0,8},{8,16},{16,24},{1,9},{9,17},{17,25},{2,10},{10,18},{18,26},{... | collective-permute-start | bytes 393224 | tf_op jit(solution)/shard_map/ppermute | solution.py:18
  47.4 1.5 %collective-permute-start.1 = (bf16[8,8,8,128]{3,2,1,0:T(8,128)(2,1)S(1)}, bf16[8,8,8,128]{3,2,1,0:T(8,128)(2,1)S(1)}, u32[]{:S(2)}, u32[]{:S(2)}) collective-permute-start(bf16[8,8,8,128]{3,2,1,0:T(8,128)(2,1)S(1)} %get-tuple-element.69), channel_id=1, source_target_pairs={{8,0},{16,8},{24,16},{9,1},{17,9},{25,17},{10,2},{18,10},{26,18},{... | collective-permute-start | bytes 393224 | tf_op jit(solution)/shard_map/ppermute | solution.py:20
  51.5 2.8 %collective-permute-done.1 = bf16[8,8,8,128]{3,2,1,0:T(8,128)(2,1)S(1)} collective-permute-done((bf16[8,8,8,128]{3,2,1,0:T(8,128)(2,1)S(1)}, bf16[8,8,8,128]{3,2,1,0:T(8,128)(2,1)S(1)}, u32[]{:S(2)}, u32[]{:S(2)}) %collective-permute-start.1) | collective-permute-done | bytes 131104 | tf_op jit(solution)/shard_map/ppermute | solution.py:20
  54.4 1.1 %fusion.12 = (bf16[64,1,80,80]{3,2,0,1:T(8,128)(2,1)S(1)}, bf16[64,1,80,80]{3,2,0,1:T(8,128)(2,1)S(1)}) fusion(s32[]{:T(128)S(6)} %select_n.137, bf16[64,80,128]{2,1,0:T(8,128)(2,1)S(1)} %bitcast.101, s32[]{:T(128)S(6)} %select_n.138), kind=kLoop, calls=%fused_computation.37 | loop fusion | bytes 2949128 | tf_op jit(solution)/shard_map/stack | solution.py:133
  55.5 2.1 %pad_maximum_fusion = bf16[64,2,80,80]{3,2,0,1:T(8,128)(2,1)} fusion(bf16[64,1,80,80]{3,2,0,1:T(8,128)(2,1)S(1)} %get-tuple-element.67, bf16[64,1,80,80]{3,2,0,1:T(8,128)(2,1)S(1)} %get-tuple-element.66), kind=kLoop, calls=%fused_computation.13 | loop fusion | flops 819200 | bytes 3276800 | tf_op jit(solution)/shard_map/stack | solution.py:133
  57.6 3.5 %gather_fusion.2 = bf16[32,2,80,80]{3,2,1,0:T(8,128)(2,1)} fusion(bf16[64,2,80,80]{3,2,0,1:T(8,128)(2,1)} %pad_maximum_fusion, s32[1024]{0:T(1024)S(1)} %pad_clamp_fusion), kind=kCustom, calls=%fused_computation.2 | custom fusion | bytes 1638528 | tf_op jit(solution)/shard_map/while/body/eval_jaxpr/jit(_take)/gather | solution.py:144
  61.1 2.8 %fusion.121 = (f32[32,2]{1,0:T(8,128)S(1)}, f32[32,2,64,64]{3,2,1,0:T(8,128)S(1)}) fusion(s32[32,2,64]{2,1,0:T(2,128)S(1)} %get-tuple-element.87, bf16[32,2,80,80]{3,2,1,0:T(8,128)(2,1)} %gather_fusion.2, pred[32]{0:T(512)(128)(4,1)S(1)} %get-tuple-element.46, s32[32,2,64]{2,1,0:T(2,128)S(1)} %get-tuple-element.88), kind=kOutput, calls=%fused_computation.196 | convolution fusion | flops 96550848 | bytes 1900832 | tf_op jit(solution)/shard_map/while/body/eval_jaxpr/pcif,pcfj->pcij/dot_general | solution.py:156
  65.8 1.5 %fusion.1 = (bf16[64,64,64]{2,1,0:T(8,128)(2,1)S(1)}, bf16[64,64,64]{2,1,0:T(8,128)(2,1)S(1)}, bf16[64,64,64]{2,1,0:T(8,128)(2,1)S(1)}) fusion(bf16[64,64,128]{2,1,0:T(8,128)(2,1)S(1)} %bitcast_select_fusion, f32[64,64,128]{2,1,0:T(8,128)S(1)} %convolution_bitcast_fusion.1, f32[64,64,128]{2,1,0:T(8,128)S(1)} %convolution_bitcast_fusion), kind=kLoop, calls=%fused_computation.15 | loop fusion | flops 3145728 | bytes 6815744 | tf_op jit(solution)/shard_map/convert.8
  67.3 0.8 fusion.3
  68.1 0.8 convolution_convert_fusion
  68.9 0.9 %fusion.19 = f32[64,128,128]{2,1,0:T(8,128)S(1)} fusion(bf16[64,64,256]{2,1,0:T(8,128)(2,1)S(1)} %convolution_convert_fusion, s32[64]{0:T(128)S(1)} %compare_select_fusion.1), kind=kOutput, calls=%fused_computation.44 | convolution fusion | flops 134340608 | bytes 5243392 | tf_op jit(solution)/shard_map/while/body/eval_jaxpr/ku,bul->bkl/dot_general | solution.py:85
  69.8 1.9 %multiply_reduce_fusion.1 = (f32[64]{0:T(128)S(1)}, f32[64]{0:T(128)S(1)}, f32[64]{0:T(128)S(1)}) fusion(f32[128]{0:T(128)S(1)} %fusion.89, f32[64,128,128]{2,1,0:T(8,128)S(1)} %fusion.19, s32[64]{0:T(128)S(1)} %compare_select_fusion.1, bf16[64,64,256]{2,1,0:T(8,128)(2,1)S(1)} %convolution_convert_fusion), kind=kOutput, calls=%fused_computation.5 | convolution fusion | flops 141680448 | bytes 5245184 | tf_op jit(solution)/shard_map/while/body/eval_jaxpr/ku,bul->bkl/dot_general | solution.py:88
  72.3 8.1 %all-gather = f32[16,2,128]{2,1,0:T(2,128)S(1)} all-gather(f32[2,2,128]{2,1,0:T(2,128)S(1)} %fusion.63), channel_id=2, replica_groups=mesh['strip'=4,'date'=8] {'date'}, dimensions={0}, use_global_device_ids=true | all-gather | bytes 18432 | tf_op jit(solution)/shard_map/all_gather | solution.py:185
  80.5 0.7 fusion.124
  (70 shorter events, 10.1 us)
Async XLA Ops:
  0.6 79.8 %copy-start = (f32[2,2,16,128]{3,2,1,0:T(8,128)S(1)}, f32[2,2,16,128]{3,2,1,0:T(8,128)}, u32[]{:S(2)}) copy-start(f32[2,2,16,128]{3,2,1,0:T(8,128)} %param.9) | copy-start | bytes 98308
  4.4 16.4 %all-to-all-start = ((s32[8,1,8]{2,1,0:T(1,128)}), s32[8,1,8]{2,1,0:T(1,128)S(1)}, u32[]{:S(2)}, u32[]{:S(2)}) async-start(s32[8,1,8]{2,1,0:T(1,128)} %bitcast.18), calls=%async_computation | async-start | bytes 8192 | tf_op jit(solution)/shard_map/all_to_all | solution.py:119
  16.9 1.2 %copy-start.2 = (s32[32,2,2]{0,2,1:T(2,128)S(1)}, s32[32,2,2]{0,2,1:T(2,128)}, u32[]{:S(2)}) copy-start(s32[32,2,2]{0,2,1:T(2,128)} %param.14) | copy-start | bytes 1540
  16.9 1.4 %copy-start.5 = (s32[32]{0:T(128)S(1)}, s32[32]{0:T(128)}, u32[]{:S(2)}) copy-start(s32[32]{0:T(128)} %param.10) | copy-start | bytes 388
  19.0 3.3 %copy-start.1 = (bf16[16,64,128]{2,1,0:T(8,128)(2,1)S(1)}, bf16[16,64,128]{2,1,0:T(8,128)(2,1)}, u32[]{:S(2)}) copy-start(bf16[16,64,128]{2,1,0:T(8,128)(2,1)} %param.8) | copy-start | bytes 786436
  23.1 5.4 %copy-start.3 = (s32[32,1]{0,1:T(1,128)S(1)}, s32[32,1]{0,1:T(1,128)}, u32[]{:S(2)}) copy-start(s32[32,1]{0,1:T(1,128)} %param.11) | copy-start | bytes 388
  23.1 5.4 %copy-start.6 = (s32[32]{0:T(128)S(1)}, s32[32]{0:T(128)}, u32[]{:S(2)}) copy-start(s32[32]{0:T(128)} %param.12) | copy-start | bytes 388
  24.2 19.6 %all-to-all-start.1 = ((bf16[8,8,64,128]{3,2,1,0:T(8,128)(2,1)}), bf16[8,8,64,128]{3,2,1,0:T(8,128)(2,1)S(1)}, u32[]{:S(2)}, u32[]{:S(2)}) async-start(bf16[8,8,64,128]{3,2,1,0:T(8,128)(2,1)} %broadcast_select_fusion), calls=%async_computation.1 | async-start | bytes 2097152 | tf_op jit(solution)/shard_map/all_to_all | solution.py:122
  43.9 7.6 %collective-permute-start = (bf16[8,8,8,128]{3,2,1,0:T(8,128)(2,1)S(1)}, bf16[8,8,8,128]{3,2,1,0:T(8,128)(2,1)S(1)}, u32[]{:S(2)}, u32[]{:S(2)}) collective-permute-start(bf16[8,8,8,128]{3,2,1,0:T(8,128)(2,1)S(1)} %get-tuple-element.68), channel_id=1, source_target_pairs={{0,8},{8,16},{16,24},{1,9},{9,17},{17,25},{2,10},{10,18},{18,26},{... | collective-permute-start | bytes 393224 | tf_op jit(solution)/shard_map/ppermute | solution.py:18
  47.4 6.9 %collective-permute-start.1 = (bf16[8,8,8,128]{3,2,1,0:T(8,128)(2,1)S(1)}, bf16[8,8,8,128]{3,2,1,0:T(8,128)(2,1)S(1)}, u32[]{:S(2)}, u32[]{:S(2)}) collective-permute-start(bf16[8,8,8,128]{3,2,1,0:T(8,128)(2,1)S(1)} %get-tuple-element.69), channel_id=1, source_target_pairs={{8,0},{16,8},{24,16},{9,1},{17,9},{25,17},{10,2},{18,10},{26,18},{... | collective-permute-start | bytes 393224 | tf_op jit(solution)/shard_map/ppermute | solution.py:20
  72.1 9.2 %copy-start.4 = (f32[32,2,2]{0,2,1:T(2,128)}, f32[32,2,2]{0,2,1:T(2,128)S(1)}, u32[]{:S(2)}) copy-start(f32[32,2,2]{0,2,1:T(2,128)S(1)} %copy.27) | copy-start | bytes 1540
